TPU v7x, 32 devices: a whole 2x2x4 slice. The times are simulated.
32 devices in a mesh: gx: 8 (over y, x, core), gy: 4 (over z).
Axes of the slice: x: 2, y: 2, z: 4, core: 2. Of those that a mesh axis runs over, the one named last changes fastest.
Arguments:
- initial_thermal_state: float32 [64, 32, 16, 256], P('gx', 'gy'), may hold values from -4 to 4
- logarithmic_diffusivity: float32 [64, 32, 16, 256], P('gx', 'gy'), may hold values from -2 to 2
- rock_class_code: int32 [64, 32, 16], P('gx', 'gy'), may hold values from 0 to 7
- rock_class_diffusivity: float32 [8], replicated, may hold values from 0.004 to 0.016
- advection_courant: float32 [16], replicated, may hold values from 0 to 0.25
- probe_locations: int32 [1024], P(('gx', 'gy')), may hold values from 0 to 1023
- observed_readings: float32 [1024], P(('gx', 'gy')), may hold values from -4 to 4
- probe_noise_deviation: float32 [1024], P(('gx', 'gy')), may hold values from 0.1 to 1
- random_starters: int32 [256], replicated, may hold values from 0 to 65520
Outputs:
- temperature_final: float32 [64, 32, 16, 256], P('gx', 'gy')
- cond_updated: float32 [64, 32, 16, 256], P('gx', 'gy')
Inputs may be any that keep to these rules, and one draw needn't show every extreme that they name: probe_locations[j] is a cell (x' 8 + y') * 16 + z of the tile of device j // 32, devices ordered with gy fastest.
All inputs are finite; a program needn't handle non-finite values.
Results may differ from a plain program's by a relative error of at most 0.00017.
Values sent between devices are 32-bit elements; how exact they have to be, the bound alone decides.
No kernel may reach another device: no remote copies, remote signals or barrier semaphores. Data moves between devices by JAX's collectives and lax.ppermute only.
A program may use at most 64 MiB of HBM per device.

v0:
```python
import jax
import jax.numpy as jnp
from jax import lax
from jax.sharding import PartitionSpec as P

inflation = 4.0


def with_halo(cells, sides, width):
    for axis, dim in sides:
        count = lax.axis_size(axis)
        ends = count - 1
        head = lax.slice_in_dim(cells, 0, width, axis=dim)
        tail = lax.slice_in_dim(cells, cells.shape[dim] - width, cells.shape[dim], axis=dim)
        cells = jnp.concatenate(
            [
                lax.ppermute(tail, axis, [(i, (i + 1) % count) for i in range(ends)]),
                cells,
                lax.ppermute(head, axis, [((i + 1) % count, i) for i in range(ends)]),
            ],
            axis=dim,
        )
    return cells


def window(field, shift_x, shift_y, shift_z):
    return field[
        1 + shift_x : field.shape[0] - 1 + shift_x,
        1 + shift_y : field.shape[1] - 1 + shift_y,
        1 + shift_z : field.shape[2] - 1 + shift_z,
    ]


def advance_in_time(padded_temp, padded_diffusivity, advection_courant):
    temp_z = jnp.pad(padded_temp, ((0, 0), (0, 0), (1, 1), (0, 0)))
    cond_z = jnp.pad(padded_diffusivity, ((0, 0), (0, 0), (1, 1), (0, 0)))
    center = window(temp_z, 0, 0, 0)
    cond_center = window(cond_z, 0, 0, 0)
    change = jnp.zeros_like(center)
    for shift_x, shift_y, shift_z in (
        (1, 0, 0),
        (-1, 0, 0),
        (0, 1, 0),
        (0, -1, 0),
        (0, 0, 1),
        (0, 0, -1),
    ):
        change = change + 0.5 * (cond_center + window(cond_z, shift_x, shift_y, shift_z)) * (
            window(temp_z, shift_x, shift_y, shift_z) - center
        )
    upwind = center - window(temp_z, -1, 0, 0)
    return center + change - advection_courant[:, None] * upwind


def perturbation(obs_index, random_starters):
    first = random_starters * 7919 % 65521
    second = obs_index * 331 % 65521
    hashed = (first[None, :] * (second[:, None] % 32749) + first[None, :] + second[:, None]) % 65521
    uniform_value = (hashed.astype(jnp.float32) + 0.5) / 65521.0
    return jnp.sqrt(3.0) * (2.0 * uniform_value - 1.0)


def shards(
    initial_thermal_state,
    logarithmic_diffusivity,
    rock_class_code,
    rock_class_diffusivity,
    advection_courant,
    probe_locations,
    observed_readings,
    probe_noise_deviation,
    random_starters,
):
    tile_span_east, tile_span_north, stratum_indices, ensemble_roster = initial_thermal_state.shape
    levels = jnp.arange(rock_class_diffusivity.shape[0], dtype=jnp.int32)
    base_cond = jnp.sum(
        (rock_class_code[..., None] == levels).astype(jnp.float32) * rock_class_diffusivity, axis=-1
    )
    thermal_spreading_step = base_cond[..., None] * jnp.exp(logarithmic_diffusivity)
    ensemble_matrix = jnp.stack([initial_thermal_state, thermal_spreading_step])
    extended = with_halo(ensemble_matrix, (("gx", 1), ("gy", 2)), 1)
    interior_slice = advance_in_time(extended[0], extended[1], advection_courant)
    padded_middle = with_halo(interior_slice, (("gx", 0), ("gy", 1)), 1)
    final = advance_in_time(padded_middle, extended[1], advection_courant)
    flattened = final.reshape(-1, ensemble_roster)
    predicted = jnp.take(flattened, probe_locations, axis=0)
    scale = jnp.sqrt(jnp.float32(ensemble_roster - 1))
    spread = (predicted - jnp.mean(predicted, axis=1, keepdims=True)) / (
        probe_noise_deviation[:, None] * scale
    )
    obs_count = probe_locations.shape[0]
    obs_index = lax.axis_index(("gx", "gy")) * obs_count + jnp.arange(obs_count, dtype=jnp.int32)
    noise = perturbation(obs_index, random_starters)
    misfit = (
        observed_readings[:, None]
        + jnp.sqrt(inflation) * probe_noise_deviation[:, None] * noise
        - predicted
    ) / probe_noise_deviation[:, None]
    local_gram = jnp.dot(spread.T, spread, precision=lax.Precision.HIGHEST)
    local_cross = jnp.dot(spread.T, misfit, precision=lax.Precision.HIGHEST)
    gram, cross = lax.psum((local_gram, local_cross), ("gx", "gy"))
    system = gram + inflation * jnp.eye(ensemble_roster, dtype=jnp.float32)
    lower_factor = jnp.linalg.cholesky(system)
    halfway = lax.linalg.triangular_solve(lower_factor, cross, left_side=True, lower=True)
    weights = lax.linalg.triangular_solve(
        lower_factor, halfway, left_side=True, lower=True, transpose_a=True
    )
    anomalies = (
        (logarithmic_diffusivity - jnp.mean(logarithmic_diffusivity, axis=-1, keepdims=True))
        / scale
    ).reshape(-1, ensemble_roster)
    updated = logarithmic_diffusivity.reshape(-1, ensemble_roster) + jnp.dot(
        anomalies, weights, precision=lax.Precision.HIGHEST
    )
    return (final, updated.reshape(logarithmic_diffusivity.shape))


def solution(mesh):
    placed = (
        P("gx", "gy", None, None),
        P("gx", "gy", None, None),
        P("gx", "gy", None),
        P(),
        P(),
        P(("gx", "gy")),
        P(("gx", "gy")),
        P(("gx", "gy")),
        P(),
    )
    return jax.shard_map(
        shards,
        mesh=mesh,
        in_specs=placed,
        out_specs=(P("gx", "gy", None, None), P("gx", "gy", None, None)),
        check_vma=False,
    )
```

profile of v0, /device:TPU:0, one launch (start us, length us, event | category | flops | bytes accessed | tf_op | source)
XLA Modules:
  0.0 271.9 jit_solution(12888231429412441590)
XLA Ops:
  7.2 1.5 reduce_sum.28
  8.8 0.9 select_reduce_fusion
  9.7 1.6 subtract_multiply_fusion
  11.4 2.4 collective-permute-start
  13.7 1.3 collective-permute-start.1
  15.1 4.2 %collective-permute-done.1 = f32[2,1,8,16,256]{4,3,2,1,0:T(8,128)S(1)} collective-permute-done((f32[2,1,8,16,256]{4,3,2,1,0:T(8,128)S(1)}, f32[2,1,8,16,256]{4,3,2,1,0:T(8,128)S(1)}, u32[]{:S(2)}, u32[]{:S(2)}) %collective-permute-start.1) | collective-permute-done | bytes 262176 | tf_op jit(solution)/shard_map/ppermute | solution.py:19
  19.3 0.7 copy-done.3
  20.0 0.9 pad_maximum_fusion.12
  20.8 4.2 %collective-permute-start.2 = (f32[2,10,1,16,256]{4,3,2,1,0:T(8,128)}, f32[2,10,1,16,256]{4,3,2,1,0:T(8,128)}, u32[]{:S(2)}, u32[]{:S(2)}) collective-permute-start(f32[2,10,1,16,256]{4,3,2,1,0:T(8,128)} %get-tuple-element.32), channel_id=1, source_target_pairs={{0,1},{1,2},{2,3},{4,5},{5,6},{6,7},{8,9},{9,10},{10,11},{12,13},{... | collective-permute-start | bytes 983048 | tf_op jit(solution)/shard_map/ppermute | solution.py:17
  25.0 1.3 collective-permute-start.3
  26.4 2.8 %collective-permute-done.2 = f32[2,10,1,16,256]{4,3,2,1,0:T(8,128)} collective-permute-done((f32[2,10,1,16,256]{4,3,2,1,0:T(8,128)}, f32[2,10,1,16,256]{4,3,2,1,0:T(8,128)}, u32[]{:S(2)}, u32[]{:S(2)}) %collective-permute-start.2) | collective-permute-done | bytes 327712 | tf_op jit(solution)/shard_map/ppermute | solution.py:17
  29.2 5.1 %collective-permute-done.3 = f32[2,10,1,16,256]{4,3,2,1,0:T(8,128)} collective-permute-done((f32[2,10,1,16,256]{4,3,2,1,0:T(8,128)}, f32[2,10,1,16,256]{4,3,2,1,0:T(8,128)}, u32[]{:S(2)}, u32[]{:S(2)}) %collective-permute-start.3) | collective-permute-done | bytes 327712 | tf_op jit(solution)/shard_map/ppermute | solution.py:19
  34.3 1.6 pad_maximum_fusion
  36.0 0.5 slice_bitcast_fusion
  36.6 1.9 fusion.10
  38.5 1.3 collective-permute-start.4
  39.8 5.9 %collective-permute-start.5 = (f32[1,8,16,256]{3,2,1,0:T(8,128)S(1)}, f32[1,8,16,256]{3,2,1,0:T(8,128)S(1)}, u32[]{:S(2)}, u32[]{:S(2)}) collective-permute-start(f32[1,8,16,256]{3,2,1,0:T(8,128)S(1)} %get-tuple-element.40), channel_id=1, source_target_pairs={{0,4},{4,8},{8,12},{12,16},{16,20},{20,24},{24,28},{1,5},{5,9},{9,... | collective-permute-start | bytes 393224 | tf_op jit(solution)/shard_map/ppermute | solution.py:17
  45.8 0.9 collective-permute-done.5
  46.8 1.3 collective-permute-start.6
  48.1 4.6 %collective-permute-start.7 = (f32[10,1,16,256]{3,2,1,0:T(8,128)S(1)}, f32[10,1,16,256]{3,2,1,0:T(8,128)S(1)}, u32[]{:S(2)}, u32[]{:S(2)}) collective-permute-start(f32[10,1,16,256]{3,2,1,0:T(8,128)S(1)} %get-tuple-element.36), channel_id=1, source_target_pairs={{0,1},{1,2},{2,3},{4,5},{5,6},{6,7},{8,9},{9,10},{10,11},{12,13},{... | collective-permute-start | bytes 491528 | tf_op jit(solution)/shard_map/ppermute | solution.py:17
  52.7 1.3 collective-permute-done.6
  54.0 1.5 collective-permute-done.7
  55.4 0.5 select_maximum_fusion
  55.9 2.1 fusion.16
  58.1 0.6 gather_fusion
  58.9 1.2 fusion.71
  60.1 1.2 fusion.64
  61.3 137.1 %all-reduce.7.cloned.1.call-done = (f32[256,256]{1,0:T(8,128)}, f32[256,256]{0,1:T(8,128)}) async-done(((f32[256,256]{1,0:T(8,128)}, f32[256,256]{0,1:T(8,128)}), (f32[256,256]{1,0:T(8,128)}, f32[256,256]{0,1:T(8,128)})) %all-reduce.7.cloned.1.call-update) | async-done | bytes 524304 | tf_op jit(solution)/shard_map/psum | solution.py:101
  198.4 1.0 select_add_fusion
  199.5 1.0 fusion.45
  200.6 11.7 %cholesky.49 = f32[128,128]{1,0:T(8,128)S(1)} custom-call(f32[128,128]{1,0:T(8,128)S(1)} %cholesky.115), custom_call_target="Cholesky" | custom-call | tf_op jit(solution)/shard_map/jit(cholesky)/cholesky | solution.py:103
  212.3 9.8 %custom-call.16 = f32[1,128,128]{1,2,0:T(8,128)S(1)} custom-call(f32[1,128,128]{2,1,0:T(8,128)S(1)} %get-tuple-element.43), custom_call_target="InvertDiagBlocksLowerTriangular" | custom-call | tf_op jit(solution)/shard_map/jit(cholesky)/cholesky | solution.py:103
  222.3 0.3 convolution_subtract_fusion.2
  222.6 11.7 %cholesky.103 = f32[128,128]{1,0:T(8,128)S(1)} custom-call(f32[128,128]{1,0:T(8,128)S(1)} %convolution_subtract_fusion.2), custom_call_target="Cholesky" | custom-call | tf_op jit(solution)/shard_map/jit(cholesky)/cholesky | solution.py:103
  234.7 0.6 compare_reduce_fusion
  235.3 0.6 compare_reduce_fusion.1
  237.3 4.1 %while.1 = (s32[]{:T(128)}, f32[256,256]{0,1:T(8,128)S(1)}, s32[2,2]{1,0:T(2,128)S(1)}, f32[2,128,128]{2,1,0:T(8,128)S(1)}, s32[]{:T(128)}) while((s32[]{:T(128)}, f32[256,256]{0,1:T(8,128)S(1)}, s32[2,2]{1,0:T(2,128)S(1)}, f32[2,128,128]{2,1,0:T(8,128)S(1)}, s32[]{:T(128)}) %tuple.34), condition=%wide.while_cond, body=%wide.while_body.sunk | while | flops 2 | bytes 393321 | solution.py:105
  237.4 0.6 fusion.110
  237.9 1.3 dynamic-slice.7
  239.4 0.6 fusion.110
  240.0 1.3 dynamic-slice.7
  241.4 19.9 %custom-call.17 = f32[2,128,128]{1,2,0:T(8,128)S(1)} custom-call(f32[2,128,128]{2,1,0:T(8,128)S(1)} %get-tuple-element.9), custom_call_target="InvertDiagBlocksLowerTriangular" | custom-call | tf_op jit(solution)/shard_map/triangular_solve | solution.py:105
  261.3 0.3 fusion.46
  261.6 0.3 convolution_subtract_fusion.1
  262.0 0.3 fusion.53
  262.3 0.3 fusion.52
  262.6 0.3 convolution_subtract_fusion
  263.1 2.0 convolution_add_fusion
  (57 shorter events, 1.9 us)
Async XLA Ops:
  7.2 4.1 %copy-start = (f32[8,8,16,256]{3,2,1,0:T(8,128)S(1)}, f32[8,8,16,256]{3,2,1,0:T(8,128)}, u32[]{:S(2)}) copy-start(f32[8,8,16,256]{3,2,1,0:T(8,128)} %param.9) | copy-start | bytes 3145732
  7.2 191.2 %all-reduce.7.cloned.1.call-start = ((), (), s32[]{:S(2)}) async-start(), calls=%async_computation | async-start | bytes 1048576 | tf_op jit(solution)/shard_map/psum | solution.py:101
  9.7 5.4 %copy-start.8 = (f32[32]{0:T(128)S(1)}, f32[32]{0:T(128)}, u32[]{:S(2)}) copy-start(f32[32]{0:T(128)} %param.16) | copy-start | bytes 388
  11.3 15.1 %copy-start.7 = (s32[32]{0:T(128)S(1)}, s32[32]{0:T(128)}, u32[]{:S(2)}) copy-start(s32[32]{0:T(128)} %param.14) | copy-start | bytes 388
  11.3 15.1 %copy-start.6 = (s32[256]{0:T(256)S(1)}, s32[256]{0:T(256)}, u32[]{:S(2)}) copy-start(s32[256]{0:T(256)} %param.17) | copy-start | bytes 3076
  11.4 3.7 %collective-permute-start = (f32[2,1,8,16,256]{4,3,2,1,0:T(8,128)S(1)}, f32[2,1,8,16,256]{4,3,2,1,0:T(8,128)S(1)}, u32[]{:S(2)}, u32[]{:S(2)}) collective-permute-start(f32[2,1,8,16,256]{4,3,2,1,0:T(8,128)S(1)} %get-tuple-element.34), channel_id=1, source_target_pairs={{0,4},{4,8},{8,12},{12,16},{16,20},{20,24},{24,28},{1,5},{5,9},{9,... | collective-permute-start | bytes 786440 | tf_op jit(solution)/shard_map/ppermute | solution.py:17
  13.7 5.5 %collective-permute-start.1 = (f32[2,1,8,16,256]{4,3,2,1,0:T(8,128)S(1)}, f32[2,1,8,16,256]{4,3,2,1,0:T(8,128)S(1)}, u32[]{:S(2)}, u32[]{:S(2)}) collective-permute-start(f32[2,1,8,16,256]{4,3,2,1,0:T(8,128)S(1)} %get-tuple-element.35), channel_id=1, source_target_pairs={{4,0},{8,4},{12,8},{16,12},{20,16},{24,20},{28,24},{5,1},{9,5},{13... | collective-permute-start | bytes 786440 | tf_op jit(solution)/shard_map/ppermute | solution.py:19
  19.3 0.7 copy-start.3
  20.8 8.4 %collective-permute-start.2 = (f32[2,10,1,16,256]{4,3,2,1,0:T(8,128)}, f32[2,10,1,16,256]{4,3,2,1,0:T(8,128)}, u32[]{:S(2)}, u32[]{:S(2)}) collective-permute-start(f32[2,10,1,16,256]{4,3,2,1,0:T(8,128)} %get-tuple-element.32), channel_id=1, source_target_pairs={{0,1},{1,2},{2,3},{4,5},{5,6},{6,7},{8,9},{9,10},{10,11},{12,13},{... | collective-permute-start | bytes 983048 | tf_op jit(solution)/shard_map/ppermute | solution.py:17
  25.0 9.3 %collective-permute-start.3 = (f32[2,10,1,16,256]{4,3,2,1,0:T(8,128)}, f32[2,10,1,16,256]{4,3,2,1,0:T(8,128)}, u32[]{:S(2)}, u32[]{:S(2)}) collective-permute-start(f32[2,10,1,16,256]{4,3,2,1,0:T(8,128)} %get-tuple-element.33), channel_id=1, source_target_pairs={{1,0},{2,1},{3,2},{5,4},{6,5},{7,6},{9,8},{10,9},{11,10},{13,12},{... | collective-permute-start | bytes 983048 | tf_op jit(solution)/shard_map/ppermute | solution.py:19
  36.0 0.7 copy-start.5
  38.5 7.3 %collective-permute-start.4 = (f32[1,8,16,256]{3,2,1,0:T(8,128)S(1)}, f32[1,8,16,256]{3,2,1,0:T(8,128)S(1)}, u32[]{:S(2)}, u32[]{:S(2)}) collective-permute-start(f32[1,8,16,256]{3,2,1,0:T(8,128)S(1)} %get-tuple-element.41), channel_id=1, source_target_pairs={{4,0},{8,4},{12,8},{16,12},{20,16},{24,20},{28,24},{5,1},{9,5},{13... | collective-permute-start | bytes 393224 | tf_op jit(solution)/shard_map/ppermute | solution.py:19
  39.8 6.9 %collective-permute-start.5 = (f32[1,8,16,256]{3,2,1,0:T(8,128)S(1)}, f32[1,8,16,256]{3,2,1,0:T(8,128)S(1)}, u32[]{:S(2)}, u32[]{:S(2)}) collective-permute-start(f32[1,8,16,256]{3,2,1,0:T(8,128)S(1)} %get-tuple-element.40), channel_id=1, source_target_pairs={{0,4},{4,8},{8,12},{12,16},{16,20},{20,24},{24,28},{1,5},{5,9},{9,... | collective-permute-start | bytes 393224 | tf_op jit(solution)/shard_map/ppermute | solution.py:17
  46.8 7.2 %collective-permute-start.6 = (f32[10,1,16,256]{3,2,1,0:T(8,128)S(1)}, f32[10,1,16,256]{3,2,1,0:T(8,128)S(1)}, u32[]{:S(2)}, u32[]{:S(2)}) collective-permute-start(f32[10,1,16,256]{3,2,1,0:T(8,128)S(1)} %get-tuple-element.37), channel_id=1, source_target_pairs={{1,0},{2,1},{3,2},{5,4},{6,5},{7,6},{9,8},{10,9},{11,10},{13,12},{... | collective-permute-start | bytes 491528 | tf_op jit(solution)/shard_map/ppermute | solution.py:19
  48.1 7.4 %collective-permute-start.7 = (f32[10,1,16,256]{3,2,1,0:T(8,128)S(1)}, f32[10,1,16,256]{3,2,1,0:T(8,128)S(1)}, u32[]{:S(2)}, u32[]{:S(2)}) collective-permute-start(f32[10,1,16,256]{3,2,1,0:T(8,128)S(1)} %get-tuple-element.36), channel_id=1, source_target_pairs={{0,1},{1,2},{2,3},{4,5},{5,6},{6,7},{8,9},{9,10},{10,11},{12,13},{... | collective-permute-start | bytes 491528 | tf_op jit(solution)/shard_map/ppermute | solution.py:17
  55.9 4.2 %copy-start.9 = (f32[32]{0:T(128)S(1)}, f32[32]{0:T(128)}, u32[]{:S(2)}) copy-start(f32[32]{0:T(128)} %param.15) | copy-start | bytes 388
  58.1 177.9 %copy-start.2 = (f32[8,8,16,256]{3,2,1,0:T(8,128)}, f32[8,8,16,256]{3,2,1,0:T(8,128)S(1)}, u32[]{:S(2)}) copy-start(f32[8,8,16,256]{3,2,1,0:T(8,128)S(1)} %fusion.16) | copy-start | bytes 3145732
  199.5 61.8 %copy-start.4 = (f32[256,256]{1,0:T(8,128)S(1)}, f32[256,256]{1,0:T(8,128)}, u32[]{:S(2)}) copy-start(f32[256,256]{1,0:T(8,128)} %get-tuple-element.26) | copy-start | bytes 786436
  237.2 25.9 %copy-start.1 = (f32[8,8,16,256]{3,2,1,0:T(8,128)S(1)}, f32[8,8,16,256]{3,2,1,0:T(8,128)}, u32[]{:S(2)}) copy-start(f32[8,8,16,256]{3,2,1,0:T(8,128)} %param.10) | copy-start | bytes 3145732
Sparse Core Ops, SparseCore 0:
  61.4 136.9 all-reduce.6
where the time goes:
time: 272 us
  waiting for transfers between devices  153 us (56%)
  other arithmetic  67.8 us (25%)
  starting transfers between devices  22.3 us (8%)
  between operations  15.7 us (6%)
  local copies, waits for them, and re-layouts  6.53 us (2%)
  matrix products  6.52 us (2%)
    psum x1, waiting for transfers between devices, shards(): gram, cross = lax.psum((local_gram, local_cross), ('gx', 'gy'))  137 us
    another operation x7, other arithmetic, shards(): lower_factor = jnp.linalg.cholesky(system)  34.6 us
    another operation x3, other arithmetic, shards(): lax.linalg.triangular_solve(lower_factor, halfway, left_side=True, lower=...  19.9 us
    ppermute x4, starting transfers between devices, with_halo(): lax.ppermute(tail, axis, [(i, (i + 1) % count) for i in range(ends)])  17.1 us
    ppermute x4, waiting for transfers between devices, with_halo(): lax.ppermute(head, axis, [((i + 1) % count, i) for i in range(ends)])  10.6 us
  transfers between devices with their start and end apart: 9, of which 7 were waited for; matrix products, arithmetic and copies ran while one was open for 0% of the time, Pallas kernels for 0%

commit v1 on v0

--- a/solution.py
+++ b/solution.py
@@ -98,7 +98,7 @@
     ) / probe_noise_deviation[:, None]
     local_gram = jnp.dot(spread.T, spread, precision=lax.Precision.HIGHEST)
     local_cross = jnp.dot(spread.T, misfit, precision=lax.Precision.HIGHEST)
-    gram, cross = lax.psum((local_gram, local_cross), ("gx", "gy"))
+    gram, cross = lax.psum(lax.psum((local_gram, local_cross), "gy"), "gx")
     system = gram + inflation * jnp.eye(ensemble_roster, dtype=jnp.float32)
     lower_factor = jnp.linalg.cholesky(system)
     halfway = lax.linalg.triangular_solve(lower_factor, cross, left_side=True, lower=True)

time: 272 us -> 241 us (0.89)
  waiting for transfers between devices: 153 us -> 121 us
    psum x1 -> x2, waiting for transfers between devices: 137 us -> 105 us  [shards(): gram, cross = lax.psum(lax.psum((local_gram, local_cross), 'gy'), 'gx')]
  transfers between devices with their start and end apart: 9 -> 10, of which waited for: 7 -> 8; matrix products, arithmetic and copies ran while one was open for 0% -> 0% of each run, Pallas kernels for 0% -> 0%
where the time goes in v1:
time: 241 us; the launch traced here: 240 us
  waiting for transfers between devices  121 us (50%)
  other arithmetic  67.5 us (28%)
  starting transfers between devices  22.5 us (9%)
  between operations  15.9 us (7%)
  local copies, waits for them, and re-layouts  6.89 us (3%)
  matrix products  6.54 us (3%)
    psum x2, waiting for transfers between devices, shards(): gram, cross = lax.psum(lax.psum((local_gram, local_cross), 'gy'), 'gx')  105 us
    another operation x7, other arithmetic, shards(): lower_factor = jnp.linalg.cholesky(system)  34.7 us
    another operation x3, other arithmetic, shards(): lax.linalg.triangular_solve(lower_factor, halfway, left_side=True, lower=...  19.7 us
    ppermute x4, starting transfers between devices, with_halo(): lax.ppermute(tail, axis, [(i, (i + 1) % count) for i in range(ends)])  17.1 us
    ppermute x4, waiting for transfers between devices, with_halo(): lax.ppermute(head, axis, [((i + 1) % count, i) for i in range(ends)])  10.6 us
    ppermute x4, waiting for transfers between devices, with_halo(): lax.ppermute(tail, axis, [(i, (i + 1) % count) for i in range(ends)])  5.23 us
    ppermute x4, starting transfers between devices, with_halo(): lax.ppermute(head, axis, [((i + 1) % count, i) for i in range(ends)])  5.16 us
  transfers between devices with their start and end apart: 10, of which 8 were waited for; matrix products, arithmetic and copies ran while one was open for 0% of the time, Pallas kernels for 0%

profile of v1, /device:TPU:0, one launch (start us, length us, event | category | flops | bytes accessed | tf_op | source)
XLA Modules:
  0.0 240.4 jit_solution(5362680432884878012)
XLA Ops:
  7.2 1.5 reduce_sum.28
  8.8 0.9 select_reduce_fusion
  9.7 1.6 subtract_multiply_fusion
  11.4 2.4 collective-permute-start
  13.7 1.3 collective-permute-start.1
  15.1 4.2 %collective-permute-done.1 = f32[2,1,8,16,256]{4,3,2,1,0:T(8,128)S(1)} collective-permute-done((f32[2,1,8,16,256]{4,3,2,1,0:T(8,128)S(1)}, f32[2,1,8,16,256]{4,3,2,1,0:T(8,128)S(1)}, u32[]{:S(2)}, u32[]{:S(2)}) %collective-permute-start.1) | collective-permute-done | bytes 262176 | tf_op jit(solution)/shard_map/ppermute | solution.py:19
  19.3 0.7 copy-done.3
  20.0 0.9 pad_maximum_fusion.12
  20.8 4.2 %collective-permute-start.2 = (f32[2,10,1,16,256]{4,3,2,1,0:T(8,128)}, f32[2,10,1,16,256]{4,3,2,1,0:T(8,128)}, u32[]{:S(2)}, u32[]{:S(2)}) collective-permute-start(f32[2,10,1,16,256]{4,3,2,1,0:T(8,128)} %get-tuple-element.34), channel_id=1, source_target_pairs={{0,1},{1,2},{2,3},{4,5},{5,6},{6,7},{8,9},{9,10},{10,11},{12,13},{... | collective-permute-start | bytes 983048 | tf_op jit(solution)/shard_map/ppermute | solution.py:17
  25.0 1.3 collective-permute-start.3
  26.4 2.8 %collective-permute-done.2 = f32[2,10,1,16,256]{4,3,2,1,0:T(8,128)} collective-permute-done((f32[2,10,1,16,256]{4,3,2,1,0:T(8,128)}, f32[2,10,1,16,256]{4,3,2,1,0:T(8,128)}, u32[]{:S(2)}, u32[]{:S(2)}) %collective-permute-start.2) | collective-permute-done | bytes 327712 | tf_op jit(solution)/shard_map/ppermute | solution.py:17
  29.2 5.1 %collective-permute-done.3 = f32[2,10,1,16,256]{4,3,2,1,0:T(8,128)} collective-permute-done((f32[2,10,1,16,256]{4,3,2,1,0:T(8,128)}, f32[2,10,1,16,256]{4,3,2,1,0:T(8,128)}, u32[]{:S(2)}, u32[]{:S(2)}) %collective-permute-start.3) | collective-permute-done | bytes 327712 | tf_op jit(solution)/shard_map/ppermute | solution.py:19
  34.3 1.6 pad_maximum_fusion
  36.0 0.5 slice_bitcast_fusion
  36.6 1.9 fusion.10
  38.5 1.3 collective-permute-start.4
  39.8 5.9 %collective-permute-start.5 = (f32[1,8,16,256]{3,2,1,0:T(8,128)S(1)}, f32[1,8,16,256]{3,2,1,0:T(8,128)S(1)}, u32[]{:S(2)}, u32[]{:S(2)}) collective-permute-start(f32[1,8,16,256]{3,2,1,0:T(8,128)S(1)} %get-tuple-element.42), channel_id=1, source_target_pairs={{0,4},{4,8},{8,12},{12,16},{16,20},{20,24},{24,28},{1,5},{5,9},{9,... | collective-permute-start | bytes 393224 | tf_op jit(solution)/shard_map/ppermute | solution.py:17
  45.8 0.9 collective-permute-done.5
  46.8 1.3 collective-permute-start.6
  48.1 4.6 %collective-permute-start.7 = (f32[10,1,16,256]{3,2,1,0:T(8,128)S(1)}, f32[10,1,16,256]{3,2,1,0:T(8,128)S(1)}, u32[]{:S(2)}, u32[]{:S(2)}) collective-permute-start(f32[10,1,16,256]{3,2,1,0:T(8,128)S(1)} %get-tuple-element.38), channel_id=1, source_target_pairs={{0,1},{1,2},{2,3},{4,5},{5,6},{6,7},{8,9},{9,10},{10,11},{12,13},{... | collective-permute-start | bytes 491528 | tf_op jit(solution)/shard_map/ppermute | solution.py:17
  52.7 1.3 collective-permute-done.6
  54.0 1.5 collective-permute-done.7
  55.4 0.5 select_maximum_fusion
  55.9 2.0 fusion.16
  57.9 0.6 gather_fusion
  58.7 1.2 fusion.71
  59.9 1.2 fusion.64
  61.3 47.3 %all-reduce.11.cloned.1.call-done = (f32[256,256]{1,0:T(8,128)}, f32[256,256]{0,1:T(8,128)}) async-done(((f32[256,256]{1,0:T(8,128)}, f32[256,256]{0,1:T(8,128)}), (f32[256,256]{1,0:T(8,128)}, f32[256,256]{0,1:T(8,128)})) %all-reduce.11.cloned.1.call-update) | async-done | bytes 524304 | tf_op jit(solution)/shard_map/psum | solution.py:101
  108.7 57.7 %all-reduce.9.cloned.1.call-done = (f32[256,256]{1,0:T(8,128)}, f32[256,256]{0,1:T(8,128)}) async-done(((f32[256,256]{1,0:T(8,128)}, f32[256,256]{0,1:T(8,128)}), (f32[256,256]{1,0:T(8,128)}, f32[256,256]{0,1:T(8,128)})) %all-reduce.9.cloned.1.call-update) | async-done | bytes 524304 | tf_op jit(solution)/shard_map/psum | solution.py:101
  166.4 1.0 select_add_fusion
  167.5 1.0 fusion.45
  168.6 11.7 %cholesky.49 = f32[128,128]{1,0:T(8,128)S(1)} custom-call(f32[128,128]{1,0:T(8,128)S(1)} %cholesky.115), custom_call_target="Cholesky" | custom-call | tf_op jit(solution)/shard_map/jit(cholesky)/cholesky | solution.py:103
  180.3 9.8 %custom-call.16 = f32[1,128,128]{1,2,0:T(8,128)S(1)} custom-call(f32[1,128,128]{2,1,0:T(8,128)S(1)} %get-tuple-element.45), custom_call_target="InvertDiagBlocksLowerTriangular" | custom-call | tf_op jit(solution)/shard_map/jit(cholesky)/cholesky | solution.py:103
  190.3 0.3 convolution_subtract_fusion.2
  190.6 11.7 %cholesky.103 = f32[128,128]{1,0:T(8,128)S(1)} custom-call(f32[128,128]{1,0:T(8,128)S(1)} %convolution_subtract_fusion.2), custom_call_target="Cholesky" | custom-call | tf_op jit(solution)/shard_map/jit(cholesky)/cholesky | solution.py:103
  202.7 0.7 compare_reduce_fusion
  203.3 0.7 compare_reduce_fusion.1
  205.5 4.6 %while.1 = (s32[]{:T(128)}, f32[256,256]{0,1:T(8,128)S(1)}, s32[2,2]{1,0:T(2,128)S(1)}, f32[2,128,128]{2,1,0:T(8,128)S(1)}, s32[]{:T(128)}) while((s32[]{:T(128)}, f32[256,256]{0,1:T(8,128)S(1)}, s32[2,2]{1,0:T(2,128)S(1)}, f32[2,128,128]{2,1,0:T(8,128)S(1)}, s32[]{:T(128)}) %tuple.34), condition=%wide.while_cond, body=%wide.while_body.sunk | while | flops 2 | bytes 393321 | solution.py:105
  205.7 0.7 fusion.110
  206.4 1.4 dynamic-slice.7
  207.9 0.7 fusion.110
  208.6 1.4 dynamic-slice.7
  210.1 19.7 %custom-call.17 = f32[2,128,128]{1,2,0:T(8,128)S(1)} custom-call(f32[2,128,128]{2,1,0:T(8,128)S(1)} %get-tuple-element.9), custom_call_target="InvertDiagBlocksLowerTriangular" | custom-call | tf_op jit(solution)/shard_map/triangular_solve | solution.py:105
  229.8 0.3 fusion.46
  230.2 0.3 convolution_subtract_fusion.1
  230.5 0.3 fusion.53
  231.3 0.3 fusion.51
  231.6 2.0 convolution_add_fusion
  (60 shorter events, 2.4 us)
Async XLA Ops:
  7.2 4.1 %copy-start = (f32[8,8,16,256]{3,2,1,0:T(8,128)S(1)}, f32[8,8,16,256]{3,2,1,0:T(8,128)}, u32[]{:S(2)}) copy-start(f32[8,8,16,256]{3,2,1,0:T(8,128)} %param.9) | copy-start | bytes 3145732
  7.2 101.4 %all-reduce.11.cloned.1.call-start = ((), (), s32[]{:S(2)}) async-start(), calls=%async_computation.1 | async-start | bytes 1048576 | tf_op jit(solution)/shard_map/psum | solution.py:101
  9.7 5.4 %copy-start.8 = (f32[32]{0:T(128)S(1)}, f32[32]{0:T(128)}, u32[]{:S(2)}) copy-start(f32[32]{0:T(128)} %param.16) | copy-start | bytes 388
  11.3 15.1 %copy-start.7 = (s32[32]{0:T(128)S(1)}, s32[32]{0:T(128)}, u32[]{:S(2)}) copy-start(s32[32]{0:T(128)} %param.14) | copy-start | bytes 388
  11.3 15.1 %copy-start.6 = (s32[256]{0:T(256)S(1)}, s32[256]{0:T(256)}, u32[]{:S(2)}) copy-start(s32[256]{0:T(256)} %param.17) | copy-start | bytes 3076
  11.4 3.7 %collective-permute-start = (f32[2,1,8,16,256]{4,3,2,1,0:T(8,128)S(1)}, f32[2,1,8,16,256]{4,3,2,1,0:T(8,128)S(1)}, u32[]{:S(2)}, u32[]{:S(2)}) collective-permute-start(f32[2,1,8,16,256]{4,3,2,1,0:T(8,128)S(1)} %get-tuple-element.36), channel_id=1, source_target_pairs={{0,4},{4,8},{8,12},{12,16},{16,20},{20,24},{24,28},{1,5},{5,9},{9,... | collective-permute-start | bytes 786440 | tf_op jit(solution)/shard_map/ppermute | solution.py:17
  13.7 5.5 %collective-permute-start.1 = (f32[2,1,8,16,256]{4,3,2,1,0:T(8,128)S(1)}, f32[2,1,8,16,256]{4,3,2,1,0:T(8,128)S(1)}, u32[]{:S(2)}, u32[]{:S(2)}) collective-permute-start(f32[2,1,8,16,256]{4,3,2,1,0:T(8,128)S(1)} %get-tuple-element.37), channel_id=1, source_target_pairs={{4,0},{8,4},{12,8},{16,12},{20,16},{24,20},{28,24},{5,1},{9,5},{13... | collective-permute-start | bytes 786440 | tf_op jit(solution)/shard_map/ppermute | solution.py:19
  19.3 0.7 copy-start.3
  20.8 8.4 %collective-permute-start.2 = (f32[2,10,1,16,256]{4,3,2,1,0:T(8,128)}, f32[2,10,1,16,256]{4,3,2,1,0:T(8,128)}, u32[]{:S(2)}, u32[]{:S(2)}) collective-permute-start(f32[2,10,1,16,256]{4,3,2,1,0:T(8,128)} %get-tuple-element.34), channel_id=1, source_target_pairs={{0,1},{1,2},{2,3},{4,5},{5,6},{6,7},{8,9},{9,10},{10,11},{12,13},{... | collective-permute-start | bytes 983048 | tf_op jit(solution)/shard_map/ppermute | solution.py:17
  25.0 9.3 %collective-permute-start.3 = (f32[2,10,1,16,256]{4,3,2,1,0:T(8,128)}, f32[2,10,1,16,256]{4,3,2,1,0:T(8,128)}, u32[]{:S(2)}, u32[]{:S(2)}) collective-permute-start(f32[2,10,1,16,256]{4,3,2,1,0:T(8,128)} %get-tuple-element.35), channel_id=1, source_target_pairs={{1,0},{2,1},{3,2},{5,4},{6,5},{7,6},{9,8},{10,9},{11,10},{13,12},{... | collective-permute-start | bytes 983048 | tf_op jit(solution)/shard_map/ppermute | solution.py:19
  35.9 0.7 copy-start.5
  38.5 7.3 %collective-permute-start.4 = (f32[1,8,16,256]{3,2,1,0:T(8,128)S(1)}, f32[1,8,16,256]{3,2,1,0:T(8,128)S(1)}, u32[]{:S(2)}, u32[]{:S(2)}) collective-permute-start(f32[1,8,16,256]{3,2,1,0:T(8,128)S(1)} %get-tuple-element.43), channel_id=1, source_target_pairs={{4,0},{8,4},{12,8},{16,12},{20,16},{24,20},{28,24},{5,1},{9,5},{13... | collective-permute-start | bytes 393224 | tf_op jit(solution)/shard_map/ppermute | solution.py:19
  39.8 6.9 %collective-permute-start.5 = (f32[1,8,16,256]{3,2,1,0:T(8,128)S(1)}, f32[1,8,16,256]{3,2,1,0:T(8,128)S(1)}, u32[]{:S(2)}, u32[]{:S(2)}) collective-permute-start(f32[1,8,16,256]{3,2,1,0:T(8,128)S(1)} %get-tuple-element.42), channel_id=1, source_target_pairs={{0,4},{4,8},{8,12},{12,16},{16,20},{20,24},{24,28},{1,5},{5,9},{9,... | collective-permute-start | bytes 393224 | tf_op jit(solution)/shard_map/ppermute | solution.py:17
  46.8 7.2 %collective-permute-start.6 = (f32[10,1,16,256]{3,2,1,0:T(8,128)S(1)}, f32[10,1,16,256]{3,2,1,0:T(8,128)S(1)}, u32[]{:S(2)}, u32[]{:S(2)}) collective-permute-start(f32[10,1,16,256]{3,2,1,0:T(8,128)S(1)} %get-tuple-element.39), channel_id=1, source_target_pairs={{1,0},{2,1},{3,2},{5,4},{6,5},{7,6},{9,8},{10,9},{11,10},{13,12},{... | collective-permute-start | bytes 491528 | tf_op jit(solution)/shard_map/ppermute | solution.py:19
  48.1 7.4 %collective-permute-start.7 = (f32[10,1,16,256]{3,2,1,0:T(8,128)S(1)}, f32[10,1,16,256]{3,2,1,0:T(8,128)S(1)}, u32[]{:S(2)}, u32[]{:S(2)}) collective-permute-start(f32[10,1,16,256]{3,2,1,0:T(8,128)S(1)} %get-tuple-element.38), channel_id=1, source_target_pairs={{0,1},{1,2},{2,3},{4,5},{5,6},{6,7},{8,9},{9,10},{10,11},{12,13},{... | collective-permute-start | bytes 491528 | tf_op jit(solution)/shard_map/ppermute | solution.py:17
  55.9 4.0 %copy-start.9 = (f32[32]{0:T(128)S(1)}, f32[32]{0:T(128)}, u32[]{:S(2)}) copy-start(f32[32]{0:T(128)} %param.15) | copy-start | bytes 388
  57.9 144.6 %copy-start.2 = (f32[8,8,16,256]{3,2,1,0:T(8,128)}, f32[8,8,16,256]{3,2,1,0:T(8,128)S(1)}, u32[]{:S(2)}) copy-start(f32[8,8,16,256]{3,2,1,0:T(8,128)S(1)} %fusion.16) | copy-start | bytes 3145732
  61.1 105.3 %all-reduce.9.cloned.1.call-start = ((), (), s32[]{:S(2)}) async-start(), calls=%async_computation | async-start | bytes 1048576 | tf_op jit(solution)/shard_map/psum | solution.py:101
  167.5 62.3 %copy-start.4 = (f32[256,256]{1,0:T(8,128)S(1)}, f32[256,256]{1,0:T(8,128)}, u32[]{:S(2)}) copy-start(f32[256,256]{1,0:T(8,128)} %get-tuple-element.26) | copy-start | bytes 786436
  205.4 26.2 %copy-start.1 = (f32[8,8,16,256]{3,2,1,0:T(8,128)S(1)}, f32[8,8,16,256]{3,2,1,0:T(8,128)}, u32[]{:S(2)}) copy-start(f32[8,8,16,256]{3,2,1,0:T(8,128)} %param.10) | copy-start | bytes 3145732
Sparse Core Ops, SparseCore 0:
  61.2 47.3 all-reduce.10
  111.8 54.5 all-reduce.8
